TPU v7x, 512 devices: a whole 4x8x8 slice. The times are simulated.
512 devices in a mesh: grp: 8 (over y_hi, core), ctx: 64 (over x, y_lo, z).
Axes of the slice: x: 4, y: 8 (y_hi: 4, y_lo: 2; y = y_hi * 2 + y_lo), z: 8, core: 2. Of those that a mesh axis runs over, the one named last changes fastest.
Arguments:
- queries: bfloat16 [65536, 4096], P(('grp', 'ctx')), may hold values from -6 to 6
- keys: bfloat16 [65536, 512], P(('grp', 'ctx')), may hold values from -6 to 6
- values: bfloat16 [65536, 512], P(('grp', 'ctx')), may hold values from -6 to 6
- d_unit: bfloat16 [65536, 4096], P(('grp', 'ctx')), may hold values from -6 to 6
- token_terms: float32 [65536], P(('grp', 'ctx')), may hold values from -4 to 4
- spans: int32 [128, 3], P('grp'), may hold values from 1 to 3, as said below
Outputs:
- attended: bfloat16 [65536, 4096], P(('grp', 'ctx'))
- query_grad: bfloat16 [65536, 4096], P(('grp', 'ctx'))
- key_gradient: bfloat16 [65536, 512], P(('grp', 'ctx'))
- value_gradient: bfloat16 [65536, 512], P(('grp', 'ctx'))
Inputs may be any that keep to these rules, and one draw needn't show every extreme that they name: `spans`: each row's 16 examples have 3 to 5 tiles each and fill its 64 tiles exactly; every span has at least one tile; every row has an example of exactly 5 tiles.
All inputs are finite; a program needn't handle non-finite values.
Results may differ from a plain program's by a relative error of at most 0.012.
The roundings to bfloat16 on the way count: a program that leaves them out, or rounds other values in their place, can miss the bound.
Values may be sent and summed in bfloat16 or wider, within the bound.
No kernel may reach another device: no remote copies, remote signals or barrier semaphores. Data moves between devices by JAX's collectives and lax.ppermute only.
A program may use at most 128 MiB of HBM per device.

v0:
```python
from functools import partial

import jax
import jax.numpy as jnp
from jax import lax
from jax.sharding import PartitionSpec as P

QUERY_HEADS = 32
KEY_VALUE_HEADS = 4
HEAD_SIZE = 128
MAX_TILES = 5


preference_beta = 0.3


def copy_for_each(shard, axis):
    copies = jnp.broadcast_to(shard, (lax.axis_size(axis), *shard.shape))
    return lax.all_to_all(copies, axis, split_axis=0, concat_axis=0, tiled=True)


def of_everyone(shard, axis):
    return copy_for_each(shard, axis).sum(axis=0)


def from_behind(shard, axis, by):
    length = lax.axis_size(axis)
    pairs = [(i, i + by) for i in range(length) if 0 <= i + by < length]
    return lax.ppermute(shard, axis, pairs)


def tile_meta(spans_row, tile_index):
    counts = spans_row[:, 0] + spans_row[:, 1] + spans_row[:, 2]
    ends = jnp.cumsum(counts)
    starts = ends - counts
    example = jnp.sum((starts[None, :] <= tile_index[:, None]).astype(jnp.int32), axis=1) - 1
    labels = jnp.arange(spans_row.shape[0], dtype=jnp.int32)
    hits = (example[:, None] == labels[None, :]).astype(jnp.int32)
    within = tile_index - jnp.sum(hits * starts[None, :], axis=1)
    prompt = jnp.sum(hits * spans_row[None, :, 0], axis=1)
    chosen = jnp.sum(hits * spans_row[None, :, 1], axis=1)
    kind = jnp.where(within < prompt, 0, jnp.where(within < prompt + chosen, 1, 2)).astype(
        jnp.int32
    )
    return (example, kind, hits)


def per_device(queries, keys, values, d_unit, token_terms, spans):
    rows_per_tile = queries.shape[0]
    heads_per_group = QUERY_HEADS // KEY_VALUE_HEADS
    score_scale = HEAD_SIZE ** (-0.5)
    position = lax.axis_index("ctx")
    key_tiles = position - jnp.arange(MAX_TILES, dtype=jnp.int32)
    key_example, key_kind, unused_hits = tile_meta(spans, key_tiles)
    own_example, own_kind, own_hits = tile_meta(spans, jnp.reshape(position, (1,)))
    blocked = (own_kind[0] == 2) & (key_kind == 1)
    live_tiles = (key_tiles >= 0) & (key_example == own_example[0]) & jnp.logical_not(blocked)
    polarity = jnp.where(own_kind[0] == 1, 1.0, jnp.where(own_kind[0] == 2, -1.0, 0.0)).astype(
        jnp.float32
    )
    own_margin = polarity * jnp.sum(token_terms)
    member = own_hits[0].astype(jnp.float32)
    margins = of_everyone(member * own_margin, "ctx")
    batch_sum = of_everyone(jnp.sum(margins), "grp")
    center = batch_sum / (spans.shape[0] * lax.axis_size("grp"))
    weights = jax.nn.sigmoid(preference_beta * (center - margins))
    own_weight = jnp.sum(member * weights)
    key_value = jnp.stack([keys, values])
    pieces = [key_value]
    moving = key_value
    for start_shift in range(1, MAX_TILES):
        moving = from_behind(moving, "ctx", 1)
        pieces.append(moving)
    span_window = jnp.stack(pieces)
    query_heads = queries.reshape(rows_per_tile, KEY_VALUE_HEADS, heads_per_group, HEAD_SIZE)
    causal = jnp.arange(rows_per_tile)[:, None] >= jnp.arange(rows_per_tile)[None, :]
    stat_dims = (KEY_VALUE_HEADS, heads_per_group, rows_per_tile, 1)
    output_dims = (rows_per_tile, KEY_VALUE_HEADS, heads_per_group, HEAD_SIZE)

    def key_block(start_shift):
        return span_window[start_shift, 0].reshape(rows_per_tile, KEY_VALUE_HEADS, HEAD_SIZE)

    def value_block(start_shift):
        return span_window[start_shift, 1].reshape(rows_per_tile, KEY_VALUE_HEADS, HEAD_SIZE)

    def masked_scores(start_shift):
        raw = (
            jnp.einsum(
                "ihgc,jhc->hgij",
                query_heads,
                key_block(start_shift),
                preferred_element_type=jnp.float32,
            )
            * score_scale
        )
        if start_shift == 0:
            raw = jnp.where(causal, raw, -jnp.inf)
        return raw

    def block_stats(start_shift):
        score_block = masked_scores(start_shift)
        block_max = jnp.max(score_block, axis=-1, keepdims=True)
        block_total = jnp.sum(jnp.exp(score_block - block_max), axis=-1, keepdims=True)
        return (block_max, block_total)

    def empty_stats():
        return (jnp.full(stat_dims, -jnp.inf, jnp.float32), jnp.zeros(stat_dims, jnp.float32))

    stats = [block_stats(0)]
    for start_shift in range(1, MAX_TILES):
        stats.append(
            lax.cond(live_tiles[start_shift], partial(block_stats, start_shift), empty_stats)
        )
    row_max = stats[0][0]
    for pair_stats in stats[1:]:
        row_max = jnp.maximum(row_max, pair_stats[0])
    exp_total = jnp.zeros_like(row_max)
    for pair_stats in stats:
        exp_total = exp_total + pair_stats[1] * jnp.exp(pair_stats[0] - row_max)
    lse = row_max + jnp.log(exp_total)

    def forward_block(start_shift):
        rounded = jnp.exp(masked_scores(start_shift) - lse).astype(jnp.bfloat16)
        return jnp.einsum(
            "hgij,jhc->ihgc", rounded, value_block(start_shift), preferred_element_type=jnp.float32
        )

    def empty_output():
        return jnp.zeros(output_dims, jnp.float32)

    output_sum = forward_block(0)
    for start_shift in range(1, MAX_TILES):
        output_sum = output_sum + lax.cond(
            live_tiles[start_shift], partial(forward_block, start_shift), empty_output
        )
    attended = output_sum.astype(jnp.bfloat16).reshape(rows_per_tile, QUERY_HEADS * HEAD_SIZE)
    output_gradient = (own_weight * d_unit.astype(jnp.float32)).astype(jnp.bfloat16)
    group_heads = output_gradient.reshape(
        rows_per_tile, KEY_VALUE_HEADS, heads_per_group, HEAD_SIZE
    )
    row_dots = jnp.transpose(
        jnp.sum(group_heads.astype(jnp.float32) * output_sum, axis=-1), (1, 2, 0)
    )[..., None]

    def backward_block(start_shift):
        probability = jnp.exp(masked_scores(start_shift) - lse)
        rounded = probability.astype(jnp.bfloat16)
        dprob = jnp.einsum(
            "ihgc,jhc->hgij",
            group_heads,
            value_block(start_shift),
            preferred_element_type=jnp.float32,
        )
        dscores = (probability * (dprob - row_dots) * score_scale).astype(jnp.bfloat16)
        query_part = jnp.einsum(
            "hgij,jhc->ihgc", dscores, key_block(start_shift), preferred_element_type=jnp.float32
        )
        key_portion = jnp.einsum(
            "hgij,ihgc->jhc", dscores, query_heads, preferred_element_type=jnp.float32
        )
        value_portion = jnp.einsum(
            "hgij,ihgc->jhc", rounded, group_heads, preferred_element_type=jnp.float32
        )
        return (
            query_part,
            jnp.stack(
                [
                    key_portion.reshape(rows_per_tile, KEY_VALUE_HEADS * HEAD_SIZE),
                    value_portion.reshape(rows_per_tile, KEY_VALUE_HEADS * HEAD_SIZE),
                ]
            ),
        )

    def empty_backward():
        return (
            jnp.zeros(output_dims, jnp.float32),
            jnp.zeros((2, rows_per_tile, KEY_VALUE_HEADS * HEAD_SIZE), jnp.float32),
        )

    query_sum, first_part = backward_block(0)
    contributions = [first_part]
    for start_shift in range(1, MAX_TILES):
        query_part, pair_part = lax.cond(
            live_tiles[start_shift], partial(backward_block, start_shift), empty_backward
        )
        query_sum = query_sum + query_part
        contributions.append(pair_part)
    contributions = jnp.stack(contributions)
    gathered = contributions[MAX_TILES - 1]
    for start_shift in range(MAX_TILES - 2, -1, -1):
        gathered = from_behind(gathered, "ctx", -1) + contributions[start_shift]
    query_grad = query_sum.astype(jnp.bfloat16).reshape(rows_per_tile, QUERY_HEADS * HEAD_SIZE)
    key_gradient = gathered[0].astype(jnp.bfloat16)
    value_gradient = gathered[1].astype(jnp.bfloat16)
    return (attended, query_grad, key_gradient, value_gradient)


def solution(mesh):
    return jax.shard_map(
        per_device,
        mesh=mesh,
        in_specs=(
            P(("grp", "ctx"), None),
            P(("grp", "ctx"), None),
            P(("grp", "ctx"), None),
            P(("grp", "ctx"), None),
            P(("grp", "ctx")),
            P("grp", None),
        ),
        out_specs=(
            P(("grp", "ctx"), None),
            P(("grp", "ctx"), None),
            P(("grp", "ctx"), None),
            P(("grp", "ctx"), None),
        ),
        check_vma=False,
    )
```

profile of v0, /device:TPU:2, one launch (start us, length us, event | category | flops | bytes accessed | tf_op | source)
XLA Modules:
  0.0 202.0 jit_solution(12268803498520558542)
XLA Ops:
  0.6 1.1 copy.357
  1.8 1.0 copy.358
  2.8 4.3 %collective-permute-start = (bf16[2,128,512]{1,2,0:T(8,128)(2,1)S(1)}, bf16[2,128,512]{1,2,0:T(8,128)(2,1)S(1)}, u32[]{:S(2)}, u32[]{:S(2)}) collective-permute-start(bf16[2,128,512]{1,2,0:T(8,128)(2,1)S(1)} %get-tuple-element.339), channel_id=1, source_target_pairs={{0,1},{1,2},{2,3},{3,4},{4,5},{5,6},{6,7},{7,8},{8,9},{9,10},{10,1... | collective-permute-start | bytes 786440 | tf_op jit(solution)/shard_map/ppermute | solution.py:29
  7.1 0.8 slice_bitcast_fusion.3
  8.2 1.4 fusion.97
  10.3 1.4 fusion.99
  14.3 1.3 reduce_sum.186
  16.9 14.0 %all-to-all-start = ((f32[64,1,16]{2,1,0:T(1,128)}), f32[64,1,16]{2,1,0:T(1,128)S(1)}, u32[]{:S(2)}, u32[]{:S(2)}) async-start(f32[64,1,16]{2,1,0:T(1,128)} %broadcast_in_dim.81), calls=%async_computation | async-start | bytes 65536 | tf_op jit(solution)/shard_map/all_to_all | solution.py:19
  30.8 0.8 fusion.101
  33.5 1.3 copy-done
  34.8 1.0 exponential_reduce_fusion
  36.0 3.4 %collective-permute-start.1 = (bf16[2,128,512]{1,2,0:T(8,128)(2,1)S(1)}, bf16[2,128,512]{1,2,0:T(8,128)(2,1)S(1)}, u32[]{:S(2)}, u32[]{:S(2)}) collective-permute-start(bf16[2,128,512]{1,2,0:T(8,128)(2,1)S(1)} %collective-permute-done), channel_id=1, source_target_pairs={{0,1},{1,2},{2,3},{3,4},{4,5},{5,6},{6,7},{7,8},{8,9},{9,10},{10,1... | collective-permute-start | bytes 786440 | tf_op jit(solution)/shard_map/ppermute | solution.py:29
  39.7 8.5 %collective-permute-done.1 = bf16[2,128,512]{1,2,0:T(8,128)(2,1)S(1)} collective-permute-done((bf16[2,128,512]{1,2,0:T(8,128)(2,1)S(1)}, bf16[2,128,512]{1,2,0:T(8,128)(2,1)S(1)}, u32[]{:S(2)}, u32[]{:S(2)}) %collective-permute-start.1) | collective-permute-done | bytes 262176 | tf_op jit(solution)/shard_map/ppermute | solution.py:29
  48.1 1.9 collective-permute-start.2
  50.1 0.7 fusion.116
  53.3 1.2 broadcast_in_dim.82
  54.5 6.2 %all-to-all-start.1 = ((f32[8,1,1]{2,1,0:T(1,128)}), f32[8,1,1]{2,1,0:T(1,128)S(1)}, u32[]{:S(2)}, u32[]{:S(2)}) async-start(f32[8,1,1]{2,1,0:T(1,128)} %broadcast_in_dim.82), calls=%async_computation.1 | async-start | bytes 8192 | tf_op jit(solution)/shard_map/all_to_all | solution.py:19
  61.4 7.0 %all-to-all-done.1 = f32[8,1,1]{2,1,0:T(1,128)S(1)} async-done(((f32[8,1,1]{2,1,0:T(1,128)}), f32[8,1,1]{2,1,0:T(1,128)S(1)}, u32[]{:S(2)}, u32[]{:S(2)}) %all-to-all-start.1) | async-done | bytes 64 | tf_op jit(solution)/shard_map/all_to_all | solution.py:19
  70.2 1.9 collective-permute-start.3
  72.2 2.1 %multiply_convert_fusion = bf16[128,4096]{1,0:T(8,128)(2,1)S(1)} fusion(bf16[128,4096]{1,0:T(8,128)(2,1)} %param.33, f32[]{:T(128)} %fusion.103), kind=kLoop, calls=%fused_computation.111 | loop fusion | flops 1572864 | bytes 2097156 | tf_op jit(solution)/shard_map/convert_element_type | solution.py:137
  77.1 6.7 %collective-permute-done.3 = bf16[2,128,512]{1,2,0:T(8,128)(2,1)} collective-permute-done((bf16[2,128,512]{1,2,0:T(8,128)(2,1)}, bf16[2,128,512]{1,2,0:T(8,128)(2,1)}, u32[]{:S(2)}, u32[]{:S(2)}) %collective-permute-start.3) | collective-permute-done | bytes 262176 | tf_op jit(solution)/shard_map/ppermute | solution.py:29
  84.5 0.8 fusion.89
  85.3 3.4 %fusion.82 = f32[4,128,8,128]{3,1,2,0:T(8,128)} fusion(bf16[128,4,128,1]{0,2,3,1:T(8,128)(2,1)S(1)} %bitcast.584, f32[4,8,128,128]{2,3,1,0:T(8,128)} %copy-done, f32[4,8,128]{2,1,0:T(8,128)S(1)} %bitcast.558), kind=kOutput, calls=%fused_computation.118 | convolution fusion | flops 135266304 | bytes 4341760 | tf_op jit(solution)/shard_map/hgij,jhc->ihgc/dot_general | solution.py:124
  88.7 1.6 conditional.17
  88.7 1.6 broadcast.201.clone
  90.3 1.6 conditional.16
  90.3 1.6 broadcast.199.clone
  91.8 1.6 conditional.18
  91.8 1.6 broadcast.203.clone
  93.4 1.6 conditional.19
  93.4 1.6 broadcast.205.clone
  95.0 6.4 %multiply_reduce_fusion = (f32[128,4,8]{0,2,1:T(8,128)S(1)}, bf16[128,4,8,128]{0,3,2,1:T(8,128)(2,1)}) fusion(bf16[128,4096]{0,1:T(8,128)(2,1)S(1)} %copy.379, f32[128,4,8,128]{0,3,2,1:T(8,128)} %get-tuple-element.291, f32[128,4,8,128]{0,3,2,1:T(8,128)} %get-tuple-element.290, f32[128,4,8,128]{0,3,2,1:T(8,128)} %get-tuple-element.289, ...), kind=kLoop, calls=%fused_computation.110 | loop fusion | flops 4190208 | bytes 12599296 | tf_op jit(solution)/shard_map/reduce_sum | solution.py:142
  101.3 1.6 conditional.23
  101.3 1.6 broadcast.219.clone
  102.9 1.0 copy.387
  103.9 26.0 %collective-permute-start.4 = (f32[2,128,512]{2,1,0:T(8,128)}, f32[2,128,512]{2,1,0:T(8,128)}, u32[]{:S(2)}, u32[]{:S(2)}) collective-permute-start(f32[2,128,512]{2,1,0:T(8,128)} %copy.387), channel_id=1, source_target_pairs={{1,0},{2,1},{3,2},{4,3},{5,4},{6,5},{7,6},{8,7},{9,8},{10,9},{11,1... | collective-permute-start | bytes 1572872 | tf_op jit(solution)/shard_map/ppermute | solution.py:29
  130.0 1.7 conditional.22
  130.0 1.6 broadcast.215.clone
  131.6 10.1 %collective-permute-done.4 = f32[2,128,512]{2,1,0:T(8,128)} collective-permute-done((f32[2,128,512]{2,1,0:T(8,128)}, f32[2,128,512]{2,1,0:T(8,128)}, u32[]{:S(2)}, u32[]{:S(2)}) %collective-permute-start.4) | collective-permute-done | bytes 524320 | tf_op jit(solution)/shard_map/ppermute | solution.py:29
  141.7 1.9 add.135
  143.6 7.4 %collective-permute-start.5 = (f32[2,128,512]{2,1,0:T(8,128)}, f32[2,128,512]{2,1,0:T(8,128)}, u32[]{:S(2)}, u32[]{:S(2)}) collective-permute-start(f32[2,128,512]{2,1,0:T(8,128)} %add.135), channel_id=1, source_target_pairs={{1,0},{2,1},{3,2},{4,3},{5,4},{6,5},{7,6},{8,7},{9,8},{10,9},{11,1... | collective-permute-start | bytes 1572872 | tf_op jit(solution)/shard_map/ppermute | solution.py:29
  151.0 2.5 %conditional.21 = (f32[128,4,8,128]{0,3,2,1:T(8,128)}, f32[2,128,512]{2,1,0:T(8,128)}) conditional(s32[]{:T(128)} %bitcast.143, () %tuple.114, (bf16[1,2,128,512]{2,3,1,0:T(8,128)(2,1)}, bf16[128,4,8,128]{0,3,2,1:T(8,128)(2,1)S(1)}, f32[4,8,128,1]{2,1,0,3:T(8,128)S(1)}, bf16[128,4,8,128]{0,3,2,1:T(8,128)(2,1)S(1)}, ...), branch_computations={%region_43.44_spmd, %region_44.45_spmd} | conditional | flops 675938304 | bytes 24100936 | solution.py:183
  151.1 1.6 broadcast.211.clone
  152.6 0.9 broadcast.212.clone
  153.5 2.4 %conditional.20 = (f32[128,4,8,128]{0,3,2,1:T(8,128)}, f32[2,128,512]{2,1,0:T(8,128)}) conditional(s32[]{:T(128)} %bitcast.141, () %tuple.112, (bf16[1,2,128,512]{2,3,1,0:T(8,128)(2,1)S(1)}, bf16[128,4,8,128]{0,3,2,1:T(8,128)(2,1)S(1)}, f32[4,8,128,1]{2,1,0,3:T(8,128)S(1)}, bf16[128,4,8,128]{0,3,2,1:T(8,128)(2,1)S(1)}, ...), branch_computations={%region_41.42_spmd, %region_42.43_spmd} | conditional | flops 675938304 | bytes 24625252 | solution.py:183
  153.5 1.6 broadcast.207.clone
  155.1 0.8 broadcast.208.clone
  155.9 2.3 %fusion.74 = bf16[4,8,128,128]{2,3,1,0:T(8,128)(2,1)S(1)} fusion(f32[4,8,128,128]{2,3,1,0:T(8,128)} %copy-done, bf16[128,4,128,1]{0,2,3,1:T(8,128)(2,1)} %bitcast.583, bf16[128,4,8,128]{0,3,2,1:T(8,128)(2,1)S(1)} %bitcast.556, f32[4,8,128]{2,1,0:T(8,128)} %bitcast.607, f32[4,8,128]{2,1,0:T(8,128)S(1)} %bitcast.559), kind=kOutput, calls=%fused_computation.104 | convolution fusion | flops 136839168 | bytes 4358144 | tf_op jit(solution)/shard_map/ihgc,jhc->hgij/dot_general | solution.py:148
  158.2 2.9 %collective-permute-done.5 = f32[2,128,512]{2,1,0:T(8,128)} collective-permute-done((f32[2,128,512]{2,1,0:T(8,128)}, f32[2,128,512]{2,1,0:T(8,128)}, u32[]{:S(2)}, u32[]{:S(2)}) %collective-permute-start.5) | collective-permute-done | bytes 524320 | tf_op jit(solution)/shard_map/ppermute | solution.py:29
  161.1 1.3 add.136
  162.4 8.6 %collective-permute-start.6 = (f32[2,128,512]{2,1,0:T(8,128)S(1)}, f32[2,128,512]{2,1,0:T(8,128)S(1)}, u32[]{:S(2)}, u32[]{:S(2)}) collective-permute-start(f32[2,128,512]{2,1,0:T(8,128)S(1)} %add.136), channel_id=1, source_target_pairs={{1,0},{2,1},{3,2},{4,3},{5,4},{6,5},{7,6},{8,7},{9,8},{10,9},{11,1... | collective-permute-start | bytes 1572872 | tf_op jit(solution)/shard_map/ppermute | solution.py:29
  171.0 1.7 fusion.126
  172.7 1.2 fusion.80
  173.9 4.7 %collective-permute-done.6 = f32[2,128,512]{2,1,0:T(8,128)S(1)} collective-permute-done((f32[2,128,512]{2,1,0:T(8,128)S(1)}, f32[2,128,512]{2,1,0:T(8,128)S(1)}, u32[]{:S(2)}, u32[]{:S(2)}) %collective-permute-start.6) | collective-permute-done | bytes 524320 | tf_op jit(solution)/shard_map/ppermute | solution.py:29
  178.6 0.9 add.137
  179.4 7.5 %collective-permute-start.7 = (f32[2,128,512]{2,1,0:T(8,128)}, f32[2,128,512]{2,1,0:T(8,128)}, u32[]{:S(2)}, u32[]{:S(2)}) collective-permute-start(f32[2,128,512]{2,1,0:T(8,128)} %add.137), channel_id=1, source_target_pairs={{1,0},{2,1},{3,2},{4,3},{5,4},{6,5},{7,6},{8,7},{9,8},{10,9},{11,1... | collective-permute-start | bytes 1572872 | tf_op jit(solution)/shard_map/ppermute | solution.py:29
  187.0 1.1 fusion.127
  188.1 1.1 copy.393
  189.2 1.8 copy.394
  191.0 5.5 %fusion.71 = bf16[128,4,8,128]{0,3,2,1:T(8,128)(2,1)} fusion(f32[128,4,8,128]{0,3,2,1:T(8,128)} %get-tuple-element.298, f32[128,4,8,128]{0,3,2,1:T(8,128)} %get-tuple-element.296, f32[128,4,8,128]{0,3,2,1:T(8,128)} %get-tuple-element.294, f32[128,4,8,128]{0,3,2,1:T(8,128)} %get-tuple-element.292, f32[4,128,8,128]{3,1,2,0:T(8,128)S(1)} %copy-done.2), kind=kLoop, calls=%fused_computation.100 | loop fusion | flops 2621440 | bytes 11534336 | tf_op jit(solution)/shard_map/convert_element_type | solution.py:192
  196.5 2.4 %copy.396 = bf16[128,4096]{1,0:T(8,128)(2,1)} copy(bf16[128,4096]{0,1:T(8,128)(2,1)} %bitcast.574) | data formatting | bytes 2097152
  198.9 1.3 copy.395
  200.2 1.1 fusion.79
  201.3 0.7 slice_bitcast_fusion
  (66 shorter events, 11.2 us)
Async XLA Ops:
  0.6 31.0 %copy-start.15 = (bf16[128,4096]{1,0:T(8,128)(2,1)S(1)}, bf16[128,4096]{1,0:T(8,128)(2,1)}, u32[]{:S(2)}) copy-start(bf16[128,4096]{1,0:T(8,128)(2,1)} %param.30) | copy-start | bytes 3145732
  2.8 33.2 %collective-permute-start = (bf16[2,128,512]{1,2,0:T(8,128)(2,1)S(1)}, bf16[2,128,512]{1,2,0:T(8,128)(2,1)S(1)}, u32[]{:S(2)}, u32[]{:S(2)}) collective-permute-start(bf16[2,128,512]{1,2,0:T(8,128)(2,1)S(1)} %get-tuple-element.339), channel_id=1, source_target_pairs={{0,1},{1,2},{2,3},{3,4},{4,5},{5,6},{6,7},{7,8},{8,9},{9,10},{10,1... | collective-permute-start | bytes 786440 | tf_op jit(solution)/shard_map/ppermute | solution.py:29
  16.9 35.8 %all-to-all-start = ((f32[64,1,16]{2,1,0:T(1,128)}), f32[64,1,16]{2,1,0:T(1,128)S(1)}, u32[]{:S(2)}, u32[]{:S(2)}) async-start(f32[64,1,16]{2,1,0:T(1,128)} %broadcast_in_dim.81), calls=%async_computation | async-start | bytes 65536 | tf_op jit(solution)/shard_map/all_to_all | solution.py:19
  33.5 1.3 copy-start
  33.5 36.7 %copy-start.20 = (f32[4,8,128]{2,1,0:T(8,128)}, f32[4,8,128]{2,1,0:T(8,128)S(1)}, u32[]{:S(2)}) copy-start(f32[4,8,128]{2,1,0:T(8,128)S(1)} %get-tuple-element.347) | copy-start | bytes 49156
  36.0 12.1 %collective-permute-start.1 = (bf16[2,128,512]{1,2,0:T(8,128)(2,1)S(1)}, bf16[2,128,512]{1,2,0:T(8,128)(2,1)S(1)}, u32[]{:S(2)}, u32[]{:S(2)}) collective-permute-start(bf16[2,128,512]{1,2,0:T(8,128)(2,1)S(1)} %collective-permute-done), channel_id=1, source_target_pairs={{0,1},{1,2},{2,3},{3,4},{4,5},{5,6},{6,7},{7,8},{8,9},{9,10},{10,1... | collective-permute-start | bytes 786440 | tf_op jit(solution)/shard_map/ppermute | solution.py:29
  48.1 24.0 %copy-start.7 = (bf16[2,128,512]{1,2,0:T(8,128)(2,1)}, bf16[2,128,512]{1,2,0:T(8,128)(2,1)S(1)}, u32[]{:S(2)}) copy-start(bf16[2,128,512]{1,2,0:T(8,128)(2,1)S(1)} %collective-permute-done.1) | copy-start | bytes 786436
  48.1 22.1 %collective-permute-start.2 = (bf16[2,128,512]{1,2,0:T(8,128)(2,1)S(1)}, bf16[2,128,512]{1,2,0:T(8,128)(2,1)}, u32[]{:S(2)}, u32[]{:S(2)}) collective-permute-start(bf16[2,128,512]{1,2,0:T(8,128)(2,1)S(1)} %collective-permute-done.1), channel_id=1, source_target_pairs={{0,1},{1,2},{2,3},{3,4},{4,5},{5,6},{6,7},{7,8},{8,9},{9,10},{10,1... | collective-permute-start | bytes 786440 | tf_op jit(solution)/shard_map/ppermute | solution.py:29
  54.5 13.8 %all-to-all-start.1 = ((f32[8,1,1]{2,1,0:T(1,128)}), f32[8,1,1]{2,1,0:T(1,128)S(1)}, u32[]{:S(2)}, u32[]{:S(2)}) async-start(f32[8,1,1]{2,1,0:T(1,128)} %broadcast_in_dim.82), calls=%async_computation.1 | async-start | bytes 8192 | tf_op jit(solution)/shard_map/all_to_all | solution.py:19
  70.2 13.5 %collective-permute-start.3 = (bf16[2,128,512]{1,2,0:T(8,128)(2,1)}, bf16[2,128,512]{1,2,0:T(8,128)(2,1)}, u32[]{:S(2)}, u32[]{:S(2)}) collective-permute-start(bf16[2,128,512]{1,2,0:T(8,128)(2,1)} %collective-permute-done.2), channel_id=1, source_target_pairs={{0,1},{1,2},{2,3},{3,4},{4,5},{5,6},{6,7},{7,8},{8,9},{9,10},{10,1... | collective-permute-start | bytes 786440 | tf_op jit(solution)/shard_map/ppermute | solution.py:29
  74.9 1.0 copy-start.8
  83.7 0.7 copy-start.21
  83.7 0.7 copy-start.22
  83.7 1.5 copy-start.9
  101.3 28.6 %copy-start.16 = (f32[128,4,8]{0,2,1:T(8,128)}, f32[128,4,8]{0,2,1:T(8,128)S(1)}, u32[]{:S(2)}) copy-start(f32[128,4,8]{0,2,1:T(8,128)S(1)} %get-tuple-element.306) | copy-start | bytes 49156
  103.9 37.8 %collective-permute-start.4 = (f32[2,128,512]{2,1,0:T(8,128)}, f32[2,128,512]{2,1,0:T(8,128)}, u32[]{:S(2)}, u32[]{:S(2)}) collective-permute-start(f32[2,128,512]{2,1,0:T(8,128)} %copy.387), channel_id=1, source_target_pairs={{1,0},{2,1},{3,2},{4,3},{5,4},{6,5},{7,6},{8,7},{9,8},{10,9},{11,1... | collective-permute-start | bytes 1572872 | tf_op jit(solution)/shard_map/ppermute | solution.py:29
  143.6 17.4 %collective-permute-start.5 = (f32[2,128,512]{2,1,0:T(8,128)}, f32[2,128,512]{2,1,0:T(8,128)}, u32[]{:S(2)}, u32[]{:S(2)}) collective-permute-start(f32[2,128,512]{2,1,0:T(8,128)} %add.135), channel_id=1, source_target_pairs={{1,0},{2,1},{3,2},{4,3},{5,4},{6,5},{7,6},{8,7},{9,8},{10,9},{11,1... | collective-permute-start | bytes 1572872 | tf_op jit(solution)/shard_map/ppermute | solution.py:29
  155.9 5.2 %copy-start.5 = (f32[2,128,512]{2,1,0:T(8,128)S(1)}, f32[2,128,512]{2,1,0:T(8,128)}, u32[]{:S(2)}) copy-start(f32[2,128,512]{2,1,0:T(8,128)} %get-tuple-element.295) | copy-start | bytes 1572868
  161.1 11.6 %copy-start.1 = (f32[4,8,128,128]{2,3,1,0:T(8,128)S(1)}, f32[4,8,128,128]{2,3,1,0:T(8,128)}, u32[]{:S(2)}) copy-start(f32[4,8,128,128]{2,3,1,0:T(8,128)} %copy-done) | copy-start | bytes 6291460
  162.4 16.2 %collective-permute-start.6 = (f32[2,128,512]{2,1,0:T(8,128)S(1)}, f32[2,128,512]{2,1,0:T(8,128)S(1)}, u32[]{:S(2)}, u32[]{:S(2)}) collective-permute-start(f32[2,128,512]{2,1,0:T(8,128)S(1)} %add.136), channel_id=1, source_target_pairs={{1,0},{2,1},{3,2},{4,3},{5,4},{6,5},{7,6},{8,7},{9,8},{10,9},{11,1... | collective-permute-start | bytes 1572872 | tf_op jit(solution)/shard_map/ppermute | solution.py:29
  172.7 5.9 %copy-start.6 = (f32[2,128,512]{2,1,0:T(8,128)S(1)}, f32[2,128,512]{2,1,0:T(8,128)}, u32[]{:S(2)}) copy-start(f32[2,128,512]{2,1,0:T(8,128)} %get-tuple-element.293) | copy-start | bytes 1572868
  179.4 11.5 %copy-start.2 = (f32[4,128,8,128]{3,1,2,0:T(8,128)S(1)}, f32[4,128,8,128]{3,1,2,0:T(8,128)}, u32[]{:S(2)}) copy-start(f32[4,128,8,128]{3,1,2,0:T(8,128)} %fusion.126) | copy-start | bytes 6291460
  179.4 20.7 %collective-permute-start.7 = (f32[2,128,512]{2,1,0:T(8,128)}, f32[2,128,512]{2,1,0:T(8,128)}, u32[]{:S(2)}, u32[]{:S(2)}) collective-permute-start(f32[2,128,512]{2,1,0:T(8,128)} %add.137), channel_id=1, source_target_pairs={{1,0},{2,1},{3,2},{4,3},{5,4},{6,5},{7,6},{8,7},{9,8},{10,9},{11,1... | collective-permute-start | bytes 1572872 | tf_op jit(solution)/shard_map/ppermute | solution.py:29
  196.5 2.4 %copy-start.3 = (bf16[128,4,8,128]{0,3,2,1:T(8,128)(2,1)S(1)}, bf16[128,4,8,128]{0,3,2,1:T(8,128)(2,1)}, u32[]{:S(2)}) copy-start(bf16[128,4,8,128]{0,3,2,1:T(8,128)(2,1)} %get-tuple-element.307) | copy-start | bytes 3145732
  196.5 3.7 %copy-start.14 = (f32[1,128,512]{2,1,0:T(8,128)S(1)}, f32[1,128,512]{2,1,0:T(8,128)}, u32[]{:S(2)}) copy-start(f32[1,128,512]{2,1,0:T(8,128)} %copy.394) | copy-start | bytes 786436
where the time goes:
time: 204 us; the launch traced here: 202 us
  starting transfers between devices  81.1 us (40%)
  waiting for transfers between devices  39.8 us (20%)
  local copies, waits for them, and re-layouts  33.6 us (16%)
  other arithmetic  29.2 us (14%)
  matrix products  10.2 us (5%)
  between operations  8.04 us (4%)
    ppermute x8, starting transfers between devices, from_behind(): return lax.ppermute(shard, axis, pairs)  61 us
    ppermute x8, waiting for transfers between devices, from_behind(): return lax.ppermute(shard, axis, pairs)  32.8 us
    all_to_all x2, starting transfers between devices, copy_for_each(): return lax.all_to_all(copies, axis, split_axis=0, concat_axis=0, tiled=True)  20.2 us
    another operation x20, local copies, waits for them, and re-layouts  16.8 us
    unnamed x35, local copies, waits for them, and re-layouts  8.27 us
    all_to_all x2, waiting for transfers between devices, copy_for_each(): return lax.all_to_all(copies, axis, split_axis=0, concat_axis=0, tiled=True)  6.96 us
    reduce_sum x1, other arithmetic, per_device(): jnp.sum(group_heads.astype(jnp.float32) * output_sum, axis=-1)  6.37 us
    convert_element_type x1, other arithmetic, per_device(): query_sum.astype(jnp.bfloat16)  5.51 us
  transfers between devices with their start and end apart: 10, of which 6 were waited for; matrix products, arithmetic and copies ran while one was open for 21% of the time, Pallas kernels for 0%

commit v1 on v0

v1 whole, which is shorter than its diff:
```python
import jax
import jax.numpy as jnp
from jax import lax
from jax.experimental import pallas as pl
from jax.experimental.pallas import tpu as pltpu
from jax.sharding import PartitionSpec as P

QUERY_HEADS = 32
KEY_VALUE_HEADS = 4
GROUP = QUERY_HEADS // KEY_VALUE_HEADS
HEAD_SIZE = 128
TILE = 128
MAX_TILES = 5
EXAMPLES = 16
LOW = -1e30
SCALE = HEAD_SIZE ** (-0.5)

preference_beta = 0.3


def copy_for_each(shard, axis):
    copies = jnp.broadcast_to(shard, (lax.axis_size(axis), *shard.shape))
    return lax.all_to_all(copies, axis, split_axis=0, concat_axis=0, tiled=True)


def from_behind(shard, axis, by):
    length = lax.axis_size(axis)
    pairs = [(i, i + by) for i in range(length) if 0 <= i + by < length]
    return lax.ppermute(shard, axis, pairs)


def own_place(spans, position):
    counts = spans[:, 0] + spans[:, 1] + spans[:, 2]
    ends = jnp.cumsum(counts)
    starts = ends - counts
    mine = ((starts <= position) & (position < ends)).astype(jnp.int32)
    start = jnp.sum(mine * starts)
    prompt_end = start + jnp.sum(mine * spans[:, 0])
    chosen_end = prompt_end + jnp.sum(mine * spans[:, 1])
    end = start + jnp.sum(mine * counts)
    return start, prompt_end, chosen_end, end


def own_weight(token_terms, start, prompt_end, chosen_end, end, position):
    polarity = jnp.where(
        position < prompt_end, 0.0, jnp.where(position < chosen_end, 1.0, -1.0)
    ).astype(jnp.float32)
    own_margin = polarity * jnp.sum(token_terms)
    row_margins = copy_for_each(own_margin[None], "ctx")[:, 0]
    tiles = jnp.arange(row_margins.shape[0], dtype=jnp.int32)
    inside = (tiles >= start) & (tiles < end)
    margin = jnp.sum(jnp.where(inside, row_margins, 0.0))
    total = jnp.sum(copy_for_each(jnp.sum(row_margins)[None], "grp"))
    center = total / (EXAMPLES * lax.axis_size("grp"))
    return jax.nn.sigmoid(preference_beta * (center - margin))


def dot(a, b, dims):
    return lax.dot_general(a, b, (dims, ((), ())), preferred_element_type=jnp.float32)


def attention_kernel(live_ref, weight_ref, q_ref, d_ref, *refs):
    k_refs, v_refs = refs[0:5], refs[5:10]
    att_ref, dq_ref = refs[10:12]
    dk_refs, dv_refs = refs[12:17], refs[17:22]
    q_scr, c_scr, s_scr, p_scr, m_scr, l_scr, r_scr, o_scr, g_scr = refs[22:]
    weight = weight_ref[0]
    for h in range(GROUP):
        cols = slice(h * HEAD_SIZE, (h + 1) * HEAD_SIZE)
        rows = slice(h * TILE, (h + 1) * TILE)
        q_scr[rows, :] = q_ref[:, cols]
        c_scr[rows, :] = (weight * d_ref[:, cols].astype(jnp.float32)).astype(jnp.bfloat16)

    def scores(s):
        raw = dot(k_refs[s][...], q_scr[...], ((1,), (1,))) * SCALE
        if s == 0:
            key_at = lax.broadcasted_iota(jnp.int32, raw.shape, 0)
            query_at = lax.broadcasted_iota(jnp.int32, raw.shape, 1) % TILE
            raw = jnp.where(key_at <= query_at, raw, LOW)
        s_scr[s] = raw
        top = jnp.max(raw, axis=0, keepdims=True)
        m_scr[...] = top if s == 0 else jnp.maximum(m_scr[...], top)

    def weights(s):
        grown = jnp.exp(s_scr[s] - m_scr[...])
        s_scr[s] = grown
        total = jnp.sum(grown, axis=0, keepdims=True)
        l_scr[...] = total if s == 0 else l_scr[...] + total

    def outputs(s):
        probability = s_scr[s] * l_scr[...]
        rounded = probability.astype(jnp.bfloat16)
        s_scr[s] = probability
        p = dot(v_refs[s][...], c_scr[...], ((1,), (1,)))
        p_scr[s] = p
        dots = jnp.sum(rounded.astype(jnp.float32) * p, axis=0, keepdims=True)
        r_scr[...] = dots if s == 0 else r_scr[...] + dots
        dv_refs[s][...] = dot(rounded, c_scr[...], ((1,), (0,))).astype(dv_refs[s].dtype)
        part = dot(v_refs[s][...].T, rounded, ((1,), (0,)))
        o_scr[...] = part if s == 0 else o_scr[...] + part

    def gradients(s):
        ds = (s_scr[s] * (p_scr[s] - r_scr[...]) * SCALE).astype(jnp.bfloat16)
        dk_refs[s][...] = dot(ds, q_scr[...], ((1,), (0,))).astype(dk_refs[s].dtype)
        part = dot(k_refs[s][...].T, ds, ((1,), (0,)))
        g_scr[...] = part if s == 0 else g_scr[...] + part

    def each(step):
        step(0)
        for s in range(1, MAX_TILES):
            pl.when(live_ref[s] != 0)(lambda s=s: step(s))

    each(scores)
    each(weights)
    l_scr[...] = 1.0 / l_scr[...]
    each(outputs)
    each(gradients)
    for s in range(1, MAX_TILES):

        @pl.when(live_ref[s] == 0)
        def _():
            dk_refs[s][...] = jnp.zeros_like(dk_refs[s])
            dv_refs[s][...] = jnp.zeros_like(dv_refs[s])

    for h in range(GROUP):
        cols = slice(h * HEAD_SIZE, (h + 1) * HEAD_SIZE)
        rows = slice(h * TILE, (h + 1) * TILE)
        att_ref[:, cols] = o_scr[:, rows].T.astype(jnp.bfloat16)
        dq_ref[:, cols] = g_scr[:, rows].T.astype(jnp.bfloat16)


def attention(live, weight, queries, d_unit, keys, values):
    wide = pl.BlockSpec((TILE, GROUP * HEAD_SIZE), lambda g: (0, g))
    narrow = pl.BlockSpec((TILE, HEAD_SIZE), lambda g: (0, g))
    scalars = pl.BlockSpec(memory_space=pltpu.SMEM)
    lanes = GROUP * TILE
    big = jax.ShapeDtypeStruct(queries.shape, jnp.bfloat16)
    kinds = [jnp.float32] * 4 + [jnp.bfloat16]
    parts = [jax.ShapeDtypeStruct((TILE, KEY_VALUE_HEADS * HEAD_SIZE), kind) for kind in kinds]
    out = pl.pallas_call(
        attention_kernel,
        grid=(KEY_VALUE_HEADS,),
        in_specs=[scalars, scalars, wide, wide] + [narrow] * 10,
        out_specs=[wide, wide] + [narrow] * 10,
        out_shape=[big, big] + parts + parts,
        scratch_shapes=[
            pltpu.VMEM((lanes, HEAD_SIZE), jnp.bfloat16),
            pltpu.VMEM((lanes, HEAD_SIZE), jnp.bfloat16),
            pltpu.VMEM((MAX_TILES, TILE, lanes), jnp.float32),
            pltpu.VMEM((MAX_TILES, TILE, lanes), jnp.float32),
            pltpu.VMEM((1, lanes), jnp.float32),
            pltpu.VMEM((1, lanes), jnp.float32),
            pltpu.VMEM((1, lanes), jnp.float32),
            pltpu.VMEM((HEAD_SIZE, lanes), jnp.float32),
            pltpu.VMEM((HEAD_SIZE, lanes), jnp.float32),
        ],
        cost_estimate=pl.CostEstimate(flops=4_000_000_000, bytes_accessed=8_000_000, transcendentals=2_600_000),
        name="attention",
    )(live, weight, queries, d_unit, *keys, *values)
    return out[0], out[1], out[2:7], out[7:12]


def per_device(queries, keys, values, d_unit, token_terms, spans):
    position = lax.axis_index("ctx")
    key_tiles, value_tiles = [keys], [values]
    for _ in range(1, MAX_TILES):
        key_tiles.append(from_behind(key_tiles[-1], "ctx", 1))
        value_tiles.append(from_behind(value_tiles[-1], "ctx", 1))
    start, prompt_end, chosen_end, end = own_place(spans, position)
    weight = own_weight(token_terms, start, prompt_end, chosen_end, end, position)
    tiles = position - jnp.arange(MAX_TILES, dtype=jnp.int32)
    chosen = (tiles >= prompt_end) & (tiles < chosen_end)
    blocked = (position >= chosen_end) & chosen
    live = ((tiles >= start) & jnp.logical_not(blocked)).astype(jnp.int32)
    attended, query_grad, key_parts, value_parts = attention(
        live, weight[None], queries, d_unit, key_tiles, value_tiles
    )
    key_sum, value_sum = key_parts[-1], value_parts[-1]
    for shift in range(MAX_TILES - 2, -1, -1):
        key_sum = from_behind(key_sum, "ctx", -1).astype(jnp.float32) + key_parts[shift]
        value_sum = from_behind(value_sum, "ctx", -1).astype(jnp.float32) + value_parts[shift]
        key_sum, value_sum = key_sum.astype(jnp.bfloat16), value_sum.astype(jnp.bfloat16)
    return attended, query_grad, key_sum, value_sum


def solution(mesh):
    return jax.shard_map(
        per_device,
        mesh=mesh,
        in_specs=(
            P(("grp", "ctx"), None),
            P(("grp", "ctx"), None),
            P(("grp", "ctx"), None),
            P(("grp", "ctx"), None),
            P(("grp", "ctx")),
            P("grp", None),
        ),
        out_specs=(
            P(("grp", "ctx"), None),
            P(("grp", "ctx"), None),
            P(("grp", "ctx"), None),
            P(("grp", "ctx"), None),
        ),
        check_vma=False,
    )
```

time: 204 us -> 141 us (0.69)
  the two profiles are of different devices: /device:TPU:2 before, /device:TPU:6 now
where the time goes in v1:
time: 141 us; the launch traced here: 140 us
  starting transfers between devices  77.9 us (55%)
  waiting for transfers between devices  24.9 us (18%)
  Pallas kernels  19.4 us (14%)
  other arithmetic  7.91 us (6%)
  between operations  6.26 us (4%)
  local copies, waits for them, and re-layouts  3.95 us (3%)
    ppermute x16, starting transfers between devices, from_behind(): return lax.ppermute(shard, axis, pairs)  60.5 us
    pallas_call x1, Pallas kernels, attention(): pl.pallas_call(attention_kernel, grid=(KEY_VALUE_HEADS,), in_specs=[scala...  19.4 us
    ppermute x16, waiting for transfers between devices, from_behind(): return lax.ppermute(shard, axis, pairs)  18.5 us
    all_to_all x2, starting transfers between devices, copy_for_each(): return lax.all_to_all(copies, axis, split_axis=0, concat_axis=0, tiled=True)  17.4 us
    all_to_all x2, waiting for transfers between devices, copy_for_each(): return lax.all_to_all(copies, axis, split_axis=0, concat_axis=0, tiled=True)  6.46 us
  transfers between devices with their start and end apart: 18, of which 7 were waited for; matrix products, arithmetic and copies ran while one was open for 7% of the time, Pallas kernels for 0%

profile of v1, /device:TPU:6, one launch (start us, length us, event | category | flops | bytes accessed | tf_op | source)
XLA Modules:
  0.0 140.4 jit_solution(9263067223386481013)
XLA Ops:
  0.6 4.3 %collective-permute-start = (bf16[128,512]{1,0:T(8,128)(2,1)}, bf16[128,512]{1,0:T(8,128)(2,1)S(1)}, u32[]{:S(2)}, u32[]{:S(2)}) collective-permute-start(bf16[128,512]{1,0:T(8,128)(2,1)} %refs_0_.1), channel_id=1, source_target_pairs={{0,1},{1,2},{2,3},{3,4},{4,5},{5,6},{6,7},{7,8},{8,9},{9,10},{10,1... | collective-permute-start | bytes 393224 | tf_op jit(solution)/shard_map/ppermute | solution.py:29
  4.9 4.3 %collective-permute-start.4 = (bf16[128,512]{1,0:T(8,128)(2,1)}, bf16[128,512]{1,0:T(8,128)(2,1)S(1)}, u32[]{:S(2)}, u32[]{:S(2)}) collective-permute-start(bf16[128,512]{1,0:T(8,128)(2,1)} %refs_5_.1), channel_id=1, source_target_pairs={{0,1},{1,2},{2,3},{3,4},{4,5},{5,6},{6,7},{7,8},{8,9},{9,10},{10,1... | collective-permute-start | bytes 393224 | tf_op jit(solution)/shard_map/ppermute | solution.py:29
  9.2 0.7 copy-done.7
  9.9 0.1 copy.15
  10.0 0.1 reduce.4
  10.1 7.3 %collective-permute-done.refs_1_ = bf16[128,512]{1,0:T(8,128)(2,1)S(1)} collective-permute-done((bf16[128,512]{1,0:T(8,128)(2,1)}, bf16[128,512]{1,0:T(8,128)(2,1)S(1)}, u32[]{:S(2)}, u32[]{:S(2)}) %collective-permute-start) | collective-permute-done | bytes 131104 | tf_op jit(solution)/shard_map/ppermute | solution.py:29
  17.4 1.9 %collective-permute-start.1 = (bf16[128,512]{1,0:T(8,128)(2,1)S(1)}, bf16[128,512]{1,0:T(8,128)(2,1)S(1)}, u32[]{:S(2)}, u32[]{:S(2)}) collective-permute-start(bf16[128,512]{1,0:T(8,128)(2,1)S(1)} %collective-permute-done.refs_1_), channel_id=1, source_target_pairs={{0,1},{1,2},{2,3},{3,4},{4,5},{5,6},{6,7},{7,8},{8,9},{9,10},{10,1... | collective-permute-start | bytes 393224 | tf_op jit(solution)/shard_map/ppermute | solution.py:29
  19.3 0.0 collective-permute-done.4.refs_6_
  19.4 1.9 %collective-permute-start.5 = (bf16[128,512]{1,0:T(8,128)(2,1)S(1)}, bf16[128,512]{1,0:T(8,128)(2,1)S(1)}, u32[]{:S(2)}, u32[]{:S(2)}) collective-permute-start(bf16[128,512]{1,0:T(8,128)(2,1)S(1)} %collective-permute-done.4.refs_6_), channel_id=1, source_target_pairs={{0,1},{1,2},{2,3},{3,4},{4,5},{5,6},{6,7},{7,8},{8,9},{9,10},{10,1... | collective-permute-start | bytes 393224 | tf_op jit(solution)/shard_map/ppermute | solution.py:29
  21.3 7.1 %collective-permute-done.1.refs_2_ = bf16[128,512]{1,0:T(8,128)(2,1)S(1)} collective-permute-done((bf16[128,512]{1,0:T(8,128)(2,1)S(1)}, bf16[128,512]{1,0:T(8,128)(2,1)S(1)}, u32[]{:S(2)}, u32[]{:S(2)}) %collective-permute-start.1) | collective-permute-done | bytes 131104 | tf_op jit(solution)/shard_map/ppermute | solution.py:29
  28.4 1.9 %collective-permute-start.2 = (bf16[128,512]{1,0:T(8,128)(2,1)S(1)}, bf16[128,512]{1,0:T(8,128)(2,1)S(1)}, u32[]{:S(2)}, u32[]{:S(2)}) collective-permute-start(bf16[128,512]{1,0:T(8,128)(2,1)S(1)} %collective-permute-done.1.refs_2_), channel_id=1, source_target_pairs={{0,1},{1,2},{2,3},{3,4},{4,5},{5,6},{6,7},{7,8},{8,9},{9,10},{10,1... | collective-permute-start | bytes 393224 | tf_op jit(solution)/shard_map/ppermute | solution.py:29
  30.3 0.0 collective-permute-done.5.refs_7_
  30.4 0.0 copy-start.11
  30.4 1.9 %collective-permute-start.6 = (bf16[128,512]{1,0:T(8,128)(2,1)S(1)}, bf16[128,512]{1,0:T(8,128)(2,1)S(1)}, u32[]{:S(2)}, u32[]{:S(2)}) collective-permute-start(bf16[128,512]{1,0:T(8,128)(2,1)S(1)} %collective-permute-done.5.refs_7_), channel_id=1, source_target_pairs={{0,1},{1,2},{2,3},{3,4},{4,5},{5,6},{6,7},{7,8},{8,9},{9,10},{10,1... | collective-permute-start | bytes 393224 | tf_op jit(solution)/shard_map/ppermute | solution.py:29
  32.3 0.8 select_reduce_fusion
  35.0 0.0 copy-start.16
  35.0 0.6 copy-done.16
  35.6 0.6 reduce_sum.75
  36.9 0.6 broadcast_in_dim.15
  37.5 11.2 %all-to-all-start = ((f32[64,1,1]{2,1,0:T(1,128)}), f32[64,1,1]{2,1,0:T(1,128)S(1)}, u32[]{:S(2)}, u32[]{:S(2)}) async-start(f32[64,1,1]{2,1,0:T(1,128)} %broadcast_in_dim.15), calls=%async_computation | async-start | bytes 65536 | tf_op jit(solution)/shard_map/all_to_all | solution.py:23
  48.7 1.1 and_convert_fusion.live_ref
  51.0 0.0 collective-permute-done.2.refs_3_
  51.1 3.4 %collective-permute-start.3 = (bf16[128,512]{1,0:T(8,128)(2,1)S(1)}, bf16[128,512]{1,0:T(8,128)(2,1)S(1)}, u32[]{:S(2)}, u32[]{:S(2)}) collective-permute-start(bf16[128,512]{1,0:T(8,128)(2,1)S(1)} %collective-permute-done.2.refs_3_), channel_id=1, source_target_pairs={{0,1},{1,2},{2,3},{3,4},{4,5},{5,6},{6,7},{7,8},{8,9},{9,10},{10,1... | collective-permute-start | bytes 393224 | tf_op jit(solution)/shard_map/ppermute | solution.py:29
  54.5 0.0 collective-permute-done.6.refs_8_
  54.5 3.4 %collective-permute-start.7 = (bf16[128,512]{1,0:T(8,128)(2,1)S(1)}, bf16[128,512]{1,0:T(8,128)(2,1)S(1)}, u32[]{:S(2)}, u32[]{:S(2)}) collective-permute-start(bf16[128,512]{1,0:T(8,128)(2,1)S(1)} %collective-permute-done.6.refs_8_), channel_id=1, source_target_pairs={{0,1},{1,2},{2,3},{3,4},{4,5},{5,6},{6,7},{7,8},{8,9},{9,10},{10,1... | collective-permute-start | bytes 393224 | tf_op jit(solution)/shard_map/ppermute | solution.py:29
  57.9 0.0 all-to-all-done
  57.9 1.0 fusion.3
  58.8 1.2 broadcast_in_dim.16
  60.1 6.2 %all-to-all-start.1 = ((f32[8,1,1]{2,1,0:T(1,128)}), f32[8,1,1]{2,1,0:T(1,128)S(1)}, u32[]{:S(2)}, u32[]{:S(2)}) async-start(f32[8,1,1]{2,1,0:T(1,128)} %broadcast_in_dim.16), calls=%async_computation.1 | async-start | bytes 8192 | tf_op jit(solution)/shard_map/all_to_all | solution.py:23
  66.3 1.2 fusion.2
  67.4 6.5 %all-to-all-done.1 = f32[8,1,1]{2,1,0:T(1,128)S(1)} async-done(((f32[8,1,1]{2,1,0:T(1,128)}), f32[8,1,1]{2,1,0:T(1,128)S(1)}, u32[]{:S(2)}, u32[]{:S(2)}) %all-to-all-start.1) | async-done | bytes 64 | tf_op jit(solution)/shard_map/all_to_all | solution.py:23
  73.9 0.6 reduce_sum.77
  75.9 0.0 collective-permute-done.3.refs_4_
  75.9 0.0 collective-permute-done.7.refs_9_
  75.9 0.0 copy-start.15
  75.9 0.0 copy-done.8
  75.9 0.0 copy-done.9
  76.0 0.0 copy-done.10
  76.0 0.0 copy-done.11
  76.0 0.0 copy-done.12
  76.0 0.0 copy-done.13
  76.0 0.6 copy-done.14
  76.6 0.1 copy-done.15
  76.6 19.4 %attention.1 = (bf16[128,4096]{1,0:T(8,128)(2,1)}, bf16[128,4096]{1,0:T(8,128)(2,1)}, f32[128,512]{1,0:T(8,128)}, f32[128,512]{1,0:T(8,128)}, f32[128,512]{1,0:T...) custom-call(s32[5]{0:T(128)} %and_convert_fusion.live_ref, ...), custom_call_target="tpu_custom_call" | custom-call | flops 4000000000 | bytes 8000000 | tf_op jit(solution)/shard_map/attention/pallas_call | solution.py:140
  96.1 5.4 %collective-permute-start.8 = (bf16[128,512]{1,0:T(8,128)(2,1)}, bf16[128,512]{1,0:T(8,128)(2,1)S(1)}, u32[]{:S(2)}, u32[]{:S(2)}) collective-permute-start(bf16[128,512]{1,0:T(8,128)(2,1)} %get-tuple-element.18), channel_id=1, source_target_pairs={{1,0},{2,1},{3,2},{4,3},{5,4},{6,5},{7,6},{8,7},{9,8},{10,9},{11,1... | collective-permute-start | bytes 393224 | tf_op jit(solution)/shard_map/ppermute | solution.py:29
  101.4 1.9 %collective-permute-start.12 = (bf16[128,512]{1,0:T(8,128)(2,1)}, bf16[128,512]{1,0:T(8,128)(2,1)S(1)}, u32[]{:S(2)}, u32[]{:S(2)}) collective-permute-start(bf16[128,512]{1,0:T(8,128)(2,1)} %get-tuple-element.23), channel_id=1, source_target_pairs={{1,0},{2,1},{3,2},{4,3},{5,4},{6,5},{7,6},{8,7},{9,8},{10,9},{11,1... | collective-permute-start | bytes 393224 | tf_op jit(solution)/shard_map/ppermute | solution.py:29
  103.4 0.9 collective-permute-done.8
  104.3 1.0 add_convert_fusion.7
  105.3 7.3 %collective-permute-start.9 = (bf16[128,512]{1,0:T(8,128)(2,1)S(1)}, bf16[128,512]{1,0:T(8,128)(2,1)S(1)}, u32[]{:S(2)}, u32[]{:S(2)}) collective-permute-start(bf16[128,512]{1,0:T(8,128)(2,1)S(1)} %add_convert_fusion.7), channel_id=1, source_target_pairs={{1,0},{2,1},{3,2},{4,3},{5,4},{6,5},{7,6},{8,7},{9,8},{10,9},{11,1... | collective-permute-start | bytes 393224 | tf_op jit(solution)/shard_map/ppermute | solution.py:29
  112.5 0.0 collective-permute-done.12
  112.6 2.1 %collective-permute-start.13 = (bf16[128,512]{1,0:T(8,128)(2,1)S(1)}, bf16[128,512]{1,0:T(8,128)(2,1)S(1)}, u32[]{:S(2)}, u32[]{:S(2)}) collective-permute-start(bf16[128,512]{1,0:T(8,128)(2,1)S(1)} %add_convert_fusion.3), channel_id=1, source_target_pairs={{1,0},{2,1},{3,2},{4,3},{5,4},{6,5},{7,6},{8,7},{9,8},{10,9},{11,1... | collective-permute-start | bytes 393224 | tf_op jit(solution)/shard_map/ppermute | solution.py:29
  114.7 0.4 collective-permute-done.9
  115.1 7.5 %collective-permute-start.10 = (bf16[128,512]{1,0:T(8,128)(2,1)S(1)}, bf16[128,512]{1,0:T(8,128)(2,1)S(1)}, u32[]{:S(2)}, u32[]{:S(2)}) collective-permute-start(bf16[128,512]{1,0:T(8,128)(2,1)S(1)} %add_convert_fusion.6), channel_id=1, source_target_pairs={{1,0},{2,1},{3,2},{4,3},{5,4},{6,5},{7,6},{8,7},{9,8},{10,9},{11,1... | collective-permute-start | bytes 393224 | tf_op jit(solution)/shard_map/ppermute | solution.py:29
  122.6 0.0 collective-permute-done.13
  122.6 0.0 copy-done.4
  122.7 2.3 %collective-permute-start.14 = (bf16[128,512]{1,0:T(8,128)(2,1)S(1)}, bf16[128,512]{1,0:T(8,128)(2,1)S(1)}, u32[]{:S(2)}, u32[]{:S(2)}) collective-permute-start(bf16[128,512]{1,0:T(8,128)(2,1)S(1)} %add_convert_fusion.2), channel_id=1, source_target_pairs={{1,0},{2,1},{3,2},{4,3},{5,4},{6,5},{7,6},{8,7},{9,8},{10,9},{11,1... | collective-permute-start | bytes 393224 | tf_op jit(solution)/shard_map/ppermute | solution.py:29
  124.9 0.1 collective-permute-done.10
  125.1 7.5 %collective-permute-start.11 = (bf16[128,512]{1,0:T(8,128)(2,1)S(1)}, bf16[128,512]{1,0:T(8,128)(2,1)S(1)}, u32[]{:S(2)}, u32[]{:S(2)}) collective-permute-start(bf16[128,512]{1,0:T(8,128)(2,1)S(1)} %add_convert_fusion.5), channel_id=1, source_target_pairs={{1,0},{2,1},{3,2},{4,3},{5,4},{6,5},{7,6},{8,7},{9,8},{10,9},{11,1... | collective-permute-start | bytes 393224 | tf_op jit(solution)/shard_map/ppermute | solution.py:29
  132.6 0.0 collective-permute-done.14
  132.7 3.6 %collective-permute-start.15 = (bf16[128,512]{1,0:T(8,128)(2,1)S(1)}, bf16[128,512]{1,0:T(8,128)(2,1)S(1)}, u32[]{:S(2)}, u32[]{:S(2)}) collective-permute-start(bf16[128,512]{1,0:T(8,128)(2,1)S(1)} %add_convert_fusion.1), channel_id=1, source_target_pairs={{1,0},{2,1},{3,2},{4,3},{5,4},{6,5},{7,6},{8,7},{9,8},{10,9},{11,1... | collective-permute-start | bytes 393224 | tf_op jit(solution)/shard_map/ppermute | solution.py:29
  136.3 0.0 collective-permute-done.11
  136.4 0.7 add_convert_fusion.4
  137.1 2.6 %collective-permute-done.15 = bf16[128,512]{1,0:T(8,128)(2,1)S(1)} collective-permute-done((bf16[128,512]{1,0:T(8,128)(2,1)S(1)}, bf16[128,512]{1,0:T(8,128)(2,1)S(1)}, u32[]{:S(2)}, u32[]{:S(2)}) %collective-permute-start.15) | collective-permute-done | bytes 131104 | tf_op jit(solution)/shard_map/ppermute | solution.py:29
  139.7 0.7 add_convert_fusion
  (28 shorter events, 0.2 us)
Async XLA Ops:
  0.6 16.8 %collective-permute-start = (bf16[128,512]{1,0:T(8,128)(2,1)}, bf16[128,512]{1,0:T(8,128)(2,1)S(1)}, u32[]{:S(2)}, u32[]{:S(2)}) collective-permute-start(bf16[128,512]{1,0:T(8,128)(2,1)} %refs_0_.1), channel_id=1, source_target_pairs={{0,1},{1,2},{2,3},{3,4},{4,5},{5,6},{6,7},{7,8},{8,9},{9,10},{10,1... | collective-permute-start | bytes 393224 | tf_op jit(solution)/shard_map/ppermute | solution.py:29
  4.9 14.4 %collective-permute-start.4 = (bf16[128,512]{1,0:T(8,128)(2,1)}, bf16[128,512]{1,0:T(8,128)(2,1)S(1)}, u32[]{:S(2)}, u32[]{:S(2)}) collective-permute-start(bf16[128,512]{1,0:T(8,128)(2,1)} %refs_5_.1), channel_id=1, source_target_pairs={{0,1},{1,2},{2,3},{3,4},{4,5},{5,6},{6,7},{7,8},{8,9},{9,10},{10,1... | collective-permute-start | bytes 393224 | tf_op jit(solution)/shard_map/ppermute | solution.py:29
  9.2 0.7 copy-start.7
  17.4 58.5 %copy-start.8 = (bf16[128,512]{1,0:T(8,128)(2,1)}, bf16[128,512]{1,0:T(8,128)(2,1)S(1)}, u32[]{:S(2)}) copy-start(bf16[128,512]{1,0:T(8,128)(2,1)S(1)} %collective-permute-done.refs_1_) | copy-start | bytes 393220
  17.4 11.0 %collective-permute-start.1 = (bf16[128,512]{1,0:T(8,128)(2,1)S(1)}, bf16[128,512]{1,0:T(8,128)(2,1)S(1)}, u32[]{:S(2)}, u32[]{:S(2)}) collective-permute-start(bf16[128,512]{1,0:T(8,128)(2,1)S(1)} %collective-permute-done.refs_1_), channel_id=1, source_target_pairs={{0,1},{1,2},{2,3},{3,4},{4,5},{5,6},{6,7},{7,8},{8,9},{9,10},{10,1... | collective-permute-start | bytes 393224 | tf_op jit(solution)/shard_map/ppermute | solution.py:29
  19.4 56.6 %copy-start.9 = (bf16[128,512]{1,0:T(8,128)(2,1)}, bf16[128,512]{1,0:T(8,128)(2,1)S(1)}, u32[]{:S(2)}) copy-start(bf16[128,512]{1,0:T(8,128)(2,1)S(1)} %collective-permute-done.4.refs_6_) | copy-start | bytes 393220
  19.4 11.0 %collective-permute-start.5 = (bf16[128,512]{1,0:T(8,128)(2,1)S(1)}, bf16[128,512]{1,0:T(8,128)(2,1)S(1)}, u32[]{:S(2)}, u32[]{:S(2)}) collective-permute-start(bf16[128,512]{1,0:T(8,128)(2,1)S(1)} %collective-permute-done.4.refs_6_), channel_id=1, source_target_pairs={{0,1},{1,2},{2,3},{3,4},{4,5},{5,6},{6,7},{7,8},{8,9},{9,10},{10,1... | collective-permute-start | bytes 393224 | tf_op jit(solution)/shard_map/ppermute | solution.py:29
  28.4 47.5 %copy-start.10 = (bf16[128,512]{1,0:T(8,128)(2,1)}, bf16[128,512]{1,0:T(8,128)(2,1)S(1)}, u32[]{:S(2)}) copy-start(bf16[128,512]{1,0:T(8,128)(2,1)S(1)} %collective-permute-done.1.refs_2_) | copy-start | bytes 393220
  28.4 22.6 %collective-permute-start.2 = (bf16[128,512]{1,0:T(8,128)(2,1)S(1)}, bf16[128,512]{1,0:T(8,128)(2,1)S(1)}, u32[]{:S(2)}, u32[]{:S(2)}) collective-permute-start(bf16[128,512]{1,0:T(8,128)(2,1)S(1)} %collective-permute-done.1.refs_2_), channel_id=1, source_target_pairs={{0,1},{1,2},{2,3},{3,4},{4,5},{5,6},{6,7},{7,8},{8,9},{9,10},{10,1... | collective-permute-start | bytes 393224 | tf_op jit(solution)/shard_map/ppermute | solution.py:29
  30.4 45.6 %copy-start.11 = (bf16[128,512]{1,0:T(8,128)(2,1)}, bf16[128,512]{1,0:T(8,128)(2,1)S(1)}, u32[]{:S(2)}) copy-start(bf16[128,512]{1,0:T(8,128)(2,1)S(1)} %collective-permute-done.5.refs_7_) | copy-start | bytes 393220
  30.4 24.1 %collective-permute-start.6 = (bf16[128,512]{1,0:T(8,128)(2,1)S(1)}, bf16[128,512]{1,0:T(8,128)(2,1)S(1)}, u32[]{:S(2)}, u32[]{:S(2)}) collective-permute-start(bf16[128,512]{1,0:T(8,128)(2,1)S(1)} %collective-permute-done.5.refs_7_), channel_id=1, source_target_pairs={{0,1},{1,2},{2,3},{3,4},{4,5},{5,6},{6,7},{7,8},{8,9},{9,10},{10,1... | collective-permute-start | bytes 393224 | tf_op jit(solution)/shard_map/ppermute | solution.py:29
  35.0 0.7 copy-start.16
  37.5 20.4 %all-to-all-start = ((f32[64,1,1]{2,1,0:T(1,128)}), f32[64,1,1]{2,1,0:T(1,128)S(1)}, u32[]{:S(2)}, u32[]{:S(2)}) async-start(f32[64,1,1]{2,1,0:T(1,128)} %broadcast_in_dim.15), calls=%async_computation | async-start | bytes 65536 | tf_op jit(solution)/shard_map/all_to_all | solution.py:23
  51.1 24.9 %copy-start.12 = (bf16[128,512]{1,0:T(8,128)(2,1)}, bf16[128,512]{1,0:T(8,128)(2,1)S(1)}, u32[]{:S(2)}) copy-start(bf16[128,512]{1,0:T(8,128)(2,1)S(1)} %collective-permute-done.2.refs_3_) | copy-start | bytes 393220
  51.1 24.8 %collective-permute-start.3 = (bf16[128,512]{1,0:T(8,128)(2,1)S(1)}, bf16[128,512]{1,0:T(8,128)(2,1)S(1)}, u32[]{:S(2)}, u32[]{:S(2)}) collective-permute-start(bf16[128,512]{1,0:T(8,128)(2,1)S(1)} %collective-permute-done.2.refs_3_), channel_id=1, source_target_pairs={{0,1},{1,2},{2,3},{3,4},{4,5},{5,6},{6,7},{7,8},{8,9},{9,10},{10,1... | collective-permute-start | bytes 393224 | tf_op jit(solution)/shard_map/ppermute | solution.py:29
  54.5 21.5 %copy-start.13 = (bf16[128,512]{1,0:T(8,128)(2,1)}, bf16[128,512]{1,0:T(8,128)(2,1)S(1)}, u32[]{:S(2)}) copy-start(bf16[128,512]{1,0:T(8,128)(2,1)S(1)} %collective-permute-done.6.refs_8_) | copy-start | bytes 393220
  54.5 21.4 %collective-permute-start.7 = (bf16[128,512]{1,0:T(8,128)(2,1)S(1)}, bf16[128,512]{1,0:T(8,128)(2,1)S(1)}, u32[]{:S(2)}, u32[]{:S(2)}) collective-permute-start(bf16[128,512]{1,0:T(8,128)(2,1)S(1)} %collective-permute-done.6.refs_8_), channel_id=1, source_target_pairs={{0,1},{1,2},{2,3},{3,4},{4,5},{5,6},{6,7},{7,8},{8,9},{9,10},{10,1... | collective-permute-start | bytes 393224 | tf_op jit(solution)/shard_map/ppermute | solution.py:29
  60.1 13.8 %all-to-all-start.1 = ((f32[8,1,1]{2,1,0:T(1,128)}), f32[8,1,1]{2,1,0:T(1,128)S(1)}, u32[]{:S(2)}, u32[]{:S(2)}) async-start(f32[8,1,1]{2,1,0:T(1,128)} %broadcast_in_dim.16), calls=%async_computation.1 | async-start | bytes 8192 | tf_op jit(solution)/shard_map/all_to_all | solution.py:23
  75.9 0.6 copy-start.14
  75.9 0.7 copy-start.15
  96.1 8.2 %collective-permute-start.8 = (bf16[128,512]{1,0:T(8,128)(2,1)}, bf16[128,512]{1,0:T(8,128)(2,1)S(1)}, u32[]{:S(2)}, u32[]{:S(2)}) collective-permute-start(bf16[128,512]{1,0:T(8,128)(2,1)} %get-tuple-element.18), channel_id=1, source_target_pairs={{1,0},{2,1},{3,2},{4,3},{5,4},{6,5},{7,6},{8,7},{9,8},{10,9},{11,1... | collective-permute-start | bytes 393224 | tf_op jit(solution)/shard_map/ppermute | solution.py:29
  101.4 11.1 %collective-permute-start.12 = (bf16[128,512]{1,0:T(8,128)(2,1)}, bf16[128,512]{1,0:T(8,128)(2,1)S(1)}, u32[]{:S(2)}, u32[]{:S(2)}) collective-permute-start(bf16[128,512]{1,0:T(8,128)(2,1)} %get-tuple-element.23), channel_id=1, source_target_pairs={{1,0},{2,1},{3,2},{4,3},{5,4},{6,5},{7,6},{8,7},{9,8},{10,9},{11,1... | collective-permute-start | bytes 393224 | tf_op jit(solution)/shard_map/ppermute | solution.py:29
  104.2 8.3 %copy-start.6 = (f32[128,512]{1,0:T(8,128)S(1)}, f32[128,512]{1,0:T(8,128)}, u32[]{:S(2)}) copy-start(f32[128,512]{1,0:T(8,128)} %get-tuple-element.24) | copy-start | bytes 786436
  105.3 9.8 %collective-permute-start.9 = (bf16[128,512]{1,0:T(8,128)(2,1)S(1)}, bf16[128,512]{1,0:T(8,128)(2,1)S(1)}, u32[]{:S(2)}, u32[]{:S(2)}) collective-permute-start(bf16[128,512]{1,0:T(8,128)(2,1)S(1)} %add_convert_fusion.7), channel_id=1, source_target_pairs={{1,0},{2,1},{3,2},{4,3},{5,4},{6,5},{7,6},{8,7},{9,8},{10,9},{11,1... | collective-permute-start | bytes 393224 | tf_op jit(solution)/shard_map/ppermute | solution.py:29
  112.6 2.5 %copy-start.5 = (f32[128,512]{1,0:T(8,128)S(1)}, f32[128,512]{1,0:T(8,128)}, u32[]{:S(2)}) copy-start(f32[128,512]{1,0:T(8,128)} %get-tuple-element.20) | copy-start | bytes 786436
  112.6 10.0 %collective-permute-start.13 = (bf16[128,512]{1,0:T(8,128)(2,1)S(1)}, bf16[128,512]{1,0:T(8,128)(2,1)S(1)}, u32[]{:S(2)}, u32[]{:S(2)}) collective-permute-start(bf16[128,512]{1,0:T(8,128)(2,1)S(1)} %add_convert_fusion.3), channel_id=1, source_target_pairs={{1,0},{2,1},{3,2},{4,3},{5,4},{6,5},{7,6},{8,7},{9,8},{10,9},{11,1... | collective-permute-start | bytes 393224 | tf_op jit(solution)/shard_map/ppermute | solution.py:29
  115.0 7.5 %copy-start.4 = (f32[128,512]{1,0:T(8,128)S(1)}, f32[128,512]{1,0:T(8,128)}, u32[]{:S(2)}) copy-start(f32[128,512]{1,0:T(8,128)} %get-tuple-element.25) | copy-start | bytes 786436
  115.1 10.0 %collective-permute-start.10 = (bf16[128,512]{1,0:T(8,128)(2,1)S(1)}, bf16[128,512]{1,0:T(8,128)(2,1)S(1)}, u32[]{:S(2)}, u32[]{:S(2)}) collective-permute-start(bf16[128,512]{1,0:T(8,128)(2,1)S(1)} %add_convert_fusion.6), channel_id=1, source_target_pairs={{1,0},{2,1},{3,2},{4,3},{5,4},{6,5},{7,6},{8,7},{9,8},{10,9},{11,1... | collective-permute-start | bytes 393224 | tf_op jit(solution)/shard_map/ppermute | solution.py:29
  122.6 2.5 %copy-start.3 = (f32[128,512]{1,0:T(8,128)S(1)}, f32[128,512]{1,0:T(8,128)}, u32[]{:S(2)}) copy-start(f32[128,512]{1,0:T(8,128)} %get-tuple-element.21) | copy-start | bytes 786436
  122.7 10.0 %collective-permute-start.14 = (bf16[128,512]{1,0:T(8,128)(2,1)S(1)}, bf16[128,512]{1,0:T(8,128)(2,1)S(1)}, u32[]{:S(2)}, u32[]{:S(2)}) collective-permute-start(bf16[128,512]{1,0:T(8,128)(2,1)S(1)} %add_convert_fusion.2), channel_id=1, source_target_pairs={{1,0},{2,1},{3,2},{4,3},{5,4},{6,5},{7,6},{8,7},{9,8},{10,9},{11,1... | collective-permute-start | bytes 393224 | tf_op jit(solution)/shard_map/ppermute | solution.py:29
  125.1 7.5 %copy-start.2 = (f32[128,512]{1,0:T(8,128)S(1)}, f32[128,512]{1,0:T(8,128)}, u32[]{:S(2)}) copy-start(f32[128,512]{1,0:T(8,128)} %get-tuple-element.26) | copy-start | bytes 786436
  125.1 11.2 %collective-permute-start.11 = (bf16[128,512]{1,0:T(8,128)(2,1)S(1)}, bf16[128,512]{1,0:T(8,128)(2,1)S(1)}, u32[]{:S(2)}, u32[]{:S(2)}) collective-permute-start(bf16[128,512]{1,0:T(8,128)(2,1)S(1)} %add_convert_fusion.5), channel_id=1, source_target_pairs={{1,0},{2,1},{3,2},{4,3},{5,4},{6,5},{7,6},{8,7},{9,8},{10,9},{11,1... | collective-permute-start | bytes 393224 | tf_op jit(solution)/shard_map/ppermute | solution.py:29
  132.6 3.7 %copy-start.1 = (f32[128,512]{1,0:T(8,128)S(1)}, f32[128,512]{1,0:T(8,128)}, u32[]{:S(2)}) copy-start(f32[128,512]{1,0:T(8,128)} %get-tuple-element.22) | copy-start | bytes 786436
  132.7 7.0 %collective-permute-start.15 = (bf16[128,512]{1,0:T(8,128)(2,1)S(1)}, bf16[128,512]{1,0:T(8,128)(2,1)S(1)}, u32[]{:S(2)}, u32[]{:S(2)}) collective-permute-start(bf16[128,512]{1,0:T(8,128)(2,1)S(1)} %add_convert_fusion.1), channel_id=1, source_target_pairs={{1,0},{2,1},{3,2},{4,3},{5,4},{6,5},{7,6},{8,7},{9,8},{10,9},{11,1... | collective-permute-start | bytes 393224 | tf_op jit(solution)/shard_map/ppermute | solution.py:29
  136.4 3.3 %copy-start = (f32[128,512]{1,0:T(8,128)S(1)}, f32[128,512]{1,0:T(8,128)}, u32[]{:S(2)}) copy-start(f32[128,512]{1,0:T(8,128)} %get-tuple-element.27) | copy-start | bytes 786436
